TPU v7x, 32 devices: a whole 2x2x4 slice. The times are simulated.
32 devices in a mesh: tile: 8 (over y, x, core), grp: 4 (over z).
Axes of the slice: x: 2, y: 2, z: 4, core: 2. Of those that a mesh axis runs over, the one named last changes fastest.
Arguments:
- amplitudes: bfloat16 [2, 64, 4096], P(None, 'tile', 'grp'), may hold values from -6 to 6
- integrals: bfloat16 [8, 16, 256, 256], P('tile', 'grp'), may hold values from -0.1875 to 0.1875
- slot_cd: int32 [8, 16], P('tile'), may hold values from 0 to 3
- slot_ab: int32 [8, 16], P('tile'), may hold values from 0 to 2, as said below
Outputs:
- ladder: bfloat16 [2, 64, 4096], P(None, 'grp', 'tile')
Inputs may be any that keep to these rules, and one draw needn't show every extreme that they name: `slot_ab`: 2 marks an empty slot. In every grid column one index of grp has all of its 4 slots live.
All inputs are finite; a program needn't handle non-finite values.
Results may differ from a plain program's by a relative error of at most 0.0085.
Values may be sent and summed in bfloat16 or wider, within the bound.
A program may use at most 64 MiB of HBM per device.

v0:
```python
import functools

import jax
import jax.numpy as jnp
from jax import lax
from jax.experimental import pallas as pl
from jax.experimental.pallas import tpu as pltpu
from jax.sharding import PartitionSpec as P

MESH = pl.DeviceIdType.MESH
NT_DEV = 2
BATCH = 2
GATHER_LIMIT = 8 * 2**20
def flip(index, mask):
    bit = 1
    while bit <= mask:
        if mask & bit:
            index = index + bit * (1 - 2 * lax.rem(lax.div(index, jnp.int32(bit)), jnp.int32(2)))
        bit *= 2
    return index


CORES = 2


def kernel(groups, places, amp_ref, int_ref, cd_ref, ab_ref, out_ref, buf, tile_buf, acc, send_buf, sums_buf, total_buf,
           cd_smem, ab_smem, local_sem, z_send, z_recv, o_send, o_recv, p_send, p_recv, c_send, c_recv, rs_send, rs_recv):
    g, t = lax.axis_index("grp"), lax.axis_index("tile")
    place, core = lax.div(t, jnp.int32(CORES)), lax.rem(t, jnp.int32(CORES))
    widths = int_ref.shape[-1]
    pairs_dev = amp_ref.shape[1]
    share = places // groups
    group = [lax.rem(g + k, groups) for k in range(groups)]
    source = [lax.rem(g - k + groups, groups) for k in range(groups)]
    spot = [flip(place, q) for q in range(places)]
    cores = (core, 1 - core)

    barrier = pltpu.get_barrier_semaphore()
    peers = [(t, group[k]) for k in range(1, groups)]
    peers += [(spot[q] * CORES + core, g) for q in range(1, places)]
    peers += [(place * CORES + 1 - core, g)]
    for peer in peers:
        pl.semaphore_signal(barrier, inc=1, device_id=peer, device_id_type=MESH)
    amp_copy = pltpu.make_async_copy(amp_ref, buf.at[g, core, place], local_sem.at[0])
    cd_copy = pltpu.make_async_copy(cd_ref, cd_smem, local_sem.at[1])
    ab_copy = pltpu.make_async_copy(ab_ref, ab_smem, local_sem.at[2])
    int_copy = pltpu.make_async_copy(int_ref, tile_buf, local_sem.at[3])
    for copy in (amp_copy, cd_copy, ab_copy, int_copy):
        copy.start()
    pl.semaphore_wait(barrier, len(peers))

    def remote(src, dst, send, recv, peer):
        copy = pltpu.make_async_remote_copy(
            src_ref=src, dst_ref=dst, send_sem=send, recv_sem=recv, device_id=peer, device_id_type=MESH)
        copy.start()
        return copy

    def spread(k):
        block = buf.at[source[k], core, place]
        return [
            remote(block, block, p_send.at[k, q - 1], p_recv.at[k, q - 1], (spot[q] * CORES + core, g))
            for q in range(1, places if k == 0 else places - 1)
        ]

    def multiply(k, part):
        j = source[k]
        cd = cd_smem[0, g * groups + j]
        ab = ab_smem[0, g * groups + j]
        operand = None
        for c in range(buf.shape[-1] // widths):
            chosen = jnp.full((1, 1, 1, widths), (cd == c).astype(jnp.float32)).astype(buf.dtype)
            block = buf[j, cores[part], :, :, :, c * widths:(c + 1) * widths] * chosen
            operand = block if operand is None else operand + block
        product = jnp.dot(operand.reshape(-1, widths), tile_buf[0, j], preferred_element_type=jnp.float32)
        product = product.reshape(*operand.shape[:3], widths)
        for a in range(NT_DEV):
            span = slice(a * widths, (a + 1) * widths)
            term = product * (ab == a).astype(jnp.float32)
            if k:
                acc[part, :, :, :, span] += term
            else:
                acc[part, :, :, :, span] = term

    def scatter(part):
        out = []
        for k in range(1, groups):
            piece = acc[part, pl.ds(group[k] * share, share)]
            send_buf[part, k - 1] = piece.astype(send_buf.dtype)
            out.append(remote(send_buf.at[part, k - 1], sums_buf.at[part, k - 1], rs_send.at[part, k - 1],
                              rs_recv.at[part, k - 1], (t, group[k])))
        return out

    amp_copy.wait()
    own = buf.at[g, core, place]
    along = [remote(own, own, z_send.at[k - 1], z_recv.at[k - 1], (t, group[k])) for k in range(1, groups)]
    spreads = [spread(0)]
    across = []
    opposite = buf.at[g, core, spot[-1]]
    for k in range(1, groups):
        along[k - 1].wait_recv()
        spreads.append(spread(k))
        if k == 1:
            spreads[0][-1].wait_recv()
            across = [remote(opposite, opposite, o_send.at[k - 1], o_recv.at[k - 1], (t, group[k])) for k in range(1, groups)]
    for copy in (cd_copy, ab_copy, int_copy):
        copy.wait()
    crossings = []
    scatters = []
    for k in range(groups):
        for copy in (spreads[0][:-1] if k == 0 else (*spreads[k], across[k - 1])):
            copy.wait_recv()
        half = buf.at[source[k], core]
        crossings.append(remote(half, half, c_send.at[k], c_recv.at[k], (place * CORES + 1 - core, g)))
        multiply(k, 0)
        if k == groups - 1:
            scatters.append(scatter(0))
        if k:
            crossings[k - 1].wait_recv()
            multiply(k - 1, 1)
    crossings[-1].wait_recv()
    multiply(groups - 1, 1)
    scatters.append(scatter(1))

    for part in range(CORES):
        total = acc[part, pl.ds(g * share, share)]
        for k in range(1, groups):
            scatters[part][k - 1].wait_recv()
            total = total + sums_buf[part, k - 1].astype(jnp.float32)
        total = (0.5 * total).astype(out_ref.dtype)
        for at in range(share):
            first = pl.multiple_of((at * CORES + cores[part]) * pairs_dev, pairs_dev)
            total_buf[:, pl.ds(first, pairs_dev), :] = total[at]
    out_copy = pltpu.make_async_copy(total_buf, out_ref, local_sem.at[0])
    out_copy.start()
    for copy in (*along, *across, *crossings, *(c for group_ in spreads + scatters for c in group_)):
        copy.wait_send()
    out_copy.wait()


def fused(groups, tiles, amplitudes, integrals, slot_cd, slot_ab):
    batch, pairs_dev, span = amplitudes.shape
    widths = integrals.shape[-1]
    places = tiles // CORES
    rows = pairs_dev * tiles // groups
    result = NT_DEV * widths
    any_spec = pl.BlockSpec(memory_space=pl.ANY)
    piece = (CORES, groups - 1, places // groups, batch, pairs_dev, result)
    dma = pltpu.SemaphoreType.DMA
    return pl.pallas_call(
        functools.partial(kernel, groups, places),
        out_shape=jax.ShapeDtypeStruct((batch, rows, result), jnp.bfloat16),
        in_specs=[any_spec] * 4,
        out_specs=any_spec,
        scratch_shapes=[
            pltpu.VMEM((groups, CORES, places, batch, pairs_dev, span), jnp.bfloat16),
            pltpu.VMEM(integrals.shape, jnp.bfloat16),
            pltpu.VMEM((CORES, places, batch, pairs_dev, result), jnp.float32),
            pltpu.VMEM(piece, jnp.bfloat16),
            pltpu.VMEM(piece, jnp.bfloat16),
            pltpu.VMEM((batch, rows, result), jnp.bfloat16),
            pltpu.SMEM(slot_cd.shape, jnp.int32),
            pltpu.SMEM(slot_ab.shape, jnp.int32),
            dma((4,)),
            dma((groups - 1,)),
            dma((groups - 1,)),
            dma((groups - 1,)),
            dma((groups - 1,)),
            dma((groups, places - 1)),
            dma((groups, places - 1)),
            dma((groups,)),
            dma((groups,)),
            dma((CORES, groups - 1)),
            dma((CORES, groups - 1)),
        ],
        compiler_params=pltpu.CompilerParams(collective_id=0, has_side_effects=True),
    )(amplitudes, integrals, slot_cd, slot_ab)


def accumulate(slot_operands, slot_tiles, ab_list):
    row_count = slot_operands.shape[0]
    widths = slot_tiles.shape[-1]
    products = jnp.einsum(
        "rsc,scd->rsd", slot_operands, slot_tiles, preferred_element_type=jnp.float32
    )
    select = (ab_list[:, None] == jnp.arange(NT_DEV, dtype=jnp.int32)[None, :]).astype(jnp.float32)
    summed = jnp.einsum("rsd,sa->rad", products, select)
    return summed.reshape(row_count, NT_DEV * widths)


def by_slabs(amplitudes, integrals, slot_cd, slot_ab):
    groups = lax.axis_size("grp")
    own_index = lax.axis_index("grp")
    widths = integrals.shape[-1]
    pairs = amplitudes.shape[1] * lax.axis_size("tile")
    cd_table = slot_cd[0].reshape(groups, groups)
    ab_table = slot_ab[0].reshape(groups, groups)
    own_tiles = integrals[0]
    moved_tiles = lax.all_to_all(own_tiles, "grp", split_axis=0, concat_axis=0, tiled=True)
    cd_list = lax.dynamic_index_in_dim(cd_table, own_index, 1, keepdims=False)
    ab_list = lax.dynamic_index_in_dim(ab_table, own_index, 1, keepdims=False)
    outputs = []
    for batch_index in range(BATCH):
        slab_block = lax.all_gather(amplitudes[batch_index], "tile", axis=0, tiled=True)
        blocks = slab_block.reshape(pairs, slab_block.shape[1] // widths, widths)
        operands = jnp.take(blocks, cd_list, axis=1)
        full_terms = accumulate(operands, moved_tiles, ab_list)
        partial_value = lax.psum_scatter(full_terms, "grp", scatter_dimension=0, tiled=True)
        outputs.append((0.5 * partial_value).astype(jnp.bfloat16))
    return jnp.stack(outputs)


def solution(mesh):
    groups, tiles = mesh.shape["grp"], mesh.shape["tile"]

    def per_device(amplitudes, integrals, slot_cd, slot_ab):
        gathered = amplitudes.size * amplitudes.dtype.itemsize * groups * tiles
        if gathered > GATHER_LIMIT or tiles % (CORES * groups) or tiles & (tiles - 1):
            return by_slabs(amplitudes, integrals, slot_cd, slot_ab)
        return fused(groups, tiles, amplitudes, integrals, slot_cd, slot_ab)

    return jax.shard_map(
        per_device,
        mesh=mesh,
        in_specs=(
            P(None, "tile", "grp"),
            P("tile", "grp", None, None),
            P("tile", None),
            P("tile", None),
        ),
        out_specs=P(None, "grp", "tile"),
        check_vma=False,
    )
```

profile of v0, /device:TPU:0, one launch (start us, length us, event | category | flops | bytes accessed | tf_op | source)
XLA Modules:
  0.0 21.7 jit_solution(7505590976934523179)
XLA Ops:
  0.0 20.3 %shard_map.46 = bf16[2,16,512]{2,1,0:T(8,128)(2,1)} custom-call(bf16[2,8,1024]{2,1,0:T(8,128)(2,1)} %amp_ref.1, bf16[1,4,256,256]{3,2,1,0:T(8,128)(2,1)} %int_ref.1, s32[1,16]{1,0:T(1,128)} %cd_ref.1, s32[1,16]{1,0:T(1,128)} %ab_ref.1), custom_call_target="tpu_custom_call" | custom-call | tf_op jit(solution)/shard_map/pallas_call | solution.py:149
  20.4 1.4 %copy.6 = bf16[2,16,512]{2,1,0:T(8,128)(2,1)} copy(bf16[2,16,512]{2,1,0:T(8,128)(2,1)} %shard_map.46) | data formatting | bytes 65536
where the time goes:
time: 21.9 us; the launch traced here: 21.7 us
  Pallas kernels  20.3 us (93%)
  local copies, waits for them, and re-layouts  1.38 us (6%)
    pallas_call x1, Pallas kernels, fused(): pl.pallas_call(functools.partial(kernel, groups, places), out_shape=jax.S...  20.3 us
    unnamed x1, local copies, waits for them, and re-layouts  1.38 us

commit v1 on v0

v1 whole, which is shorter than its diff:
```python
import functools

import jax
import jax.numpy as jnp
from jax import lax
from jax.experimental import pallas as pl
from jax.experimental.pallas import tpu as pltpu
from jax.sharding import PartitionSpec as P

MESH = pl.DeviceIdType.MESH
NT_DEV = 2
BATCH = 2
GATHER_LIMIT = 8 * 2**20
CORES = 2


def flip(index, mask):
    bit = 1
    while bit <= mask:
        if mask & bit:
            index = index + bit * (1 - 2 * lax.rem(lax.div(index, jnp.int32(bit)), jnp.int32(2)))
        bit *= 2
    return index


def farthest_first(own, count):
    low, high = jnp.int32(0), jnp.int32(count - 1)
    order = []
    for _ in range(count - 1):
        take_low = (own - low >= high - own).astype(jnp.int32)
        order.append(take_low * low + (1 - take_low) * high)
        low, high = low + take_low, high - (1 - take_low)
    return order


def kernel(groups, places, amp_ref, int_ref, cd_ref, ab_ref, out_ref, zbuf, xbuf, pbuf, abuf, sbuf, tile_buf, acc, rs_buf,
           sums_buf, cd_smem, ab_smem, amp_sem, local_sem, z_send, z_recv, t_send, t_recv, p_send, p_recv, x_send, x_recv,
           a_send, a_recv, rs_send, rs_recv):
    g, t = lax.axis_index("grp"), lax.axis_index("tile")
    place, core = lax.div(t, jnp.int32(CORES)), lax.rem(t, jnp.int32(CORES))
    widths = int_ref.shape[-1]
    tiles_dev = zbuf.shape[1]
    near = places * CORES
    spot = [flip(place, q) for q in range(places)]
    column = [spot[e // CORES] * CORES + (1 - core if e % CORES else core) for e in range(near)]
    order = farthest_first(g, groups)

    barrier = pltpu.get_barrier_semaphore()
    peers = [(t, order[k]) for k in range(groups - 1)] + [(column[e], g) for e in range(1, near)]
    for peer in peers:
        pl.semaphore_signal(barrier, inc=1, device_id=peer, device_id_type=MESH)
    amp_copies = [
        pltpu.make_async_copy(amp_ref.at[:, :, pl.ds(c * widths, widths)], zbuf.at[g, c], amp_sem.at[c])
        for c in range(tiles_dev)
    ]
    cd_copy = pltpu.make_async_copy(cd_ref, cd_smem.at[0], local_sem.at[0])
    ab_copy = pltpu.make_async_copy(ab_ref, ab_smem, local_sem.at[1])
    int_copy = pltpu.make_async_copy(int_ref, tile_buf, local_sem.at[2])
    for copy in (cd_copy, *amp_copies, ab_copy, int_copy):
        copy.start()
    pl.semaphore_wait(barrier, len(peers))

    def remote(src, dst, send, recv, peer):
        return pltpu.make_async_remote_copy(
            src_ref=src, dst_ref=dst, send_sem=send, recv_sem=recv, device_id=peer, device_id_type=MESH)

    started = []

    def send(*what):
        copy = remote(*what)
        copy.start()
        started.append(copy)
        return copy

    cd_copy.wait()
    tables = [
        send(cd_smem.at[0], cd_smem.at[e], t_send.at[e - 1], t_recv.at[e - 1], (column[e], g)) for e in range(1, near)
    ]
    for copy in amp_copies:
        copy.wait()
    for k in range(groups - 1):
        send(zbuf.at[g], zbuf.at[g], z_send.at[k], z_recv.at[g], (t, order[k]))
    blocks = [
        send(zbuf.at[g], pbuf.at[e - 1], p_send.at[e - 1], p_recv.at[e - 1], (column[e], g)) for e in range(1, near)
    ]
    ab_copy.wait()
    int_copy.wait()

    def choose(tiles, e, j):
        cd = cd_smem[e, 0, g * groups + j]
        chosen = tiles[0]
        for c in range(1, len(tiles)):
            chosen = jnp.where(cd == c, tiles[c], chosen)
        return chosen

    def load(buf, at):
        return [buf[at, c] for c in range(tiles_dev)]

    def term(parts, j):
        operand = jnp.concatenate([part.reshape(-1, widths) for part in parts], axis=0)
        product = jnp.dot(operand, tile_buf[0, j], preferred_element_type=jnp.float32)
        ab = ab_smem[0, g * groups + j]
        return [product * (ab == a).astype(jnp.float32) for a in range(NT_DEV)]

    def add(left, right):
        return [x + y for x, y in zip(left, right)]

    def finish(q, totals):
        for a in range(NT_DEV):
            acc[q, :, a * widths:(a + 1) * widths] = totals[a]
            rs_buf[q, :, a * widths:(a + 1) * widths] = totals[a].astype(rs_buf.dtype)

        @pl.when(spot[q] != g)
        def _():
            remote(rs_buf.at[q], sums_buf.at[g], rs_send.at[q], rs_recv.at[g], (t, spot[q])).start()

    blocks[0].wait_recv()
    own = term([choose(load(zbuf, g), 0, g), choose(load(pbuf, 0), 0, g)], g)
    for copy in tables:
        copy.wait_recv()
    crossings, picked = [], [[] for _ in range(places)]
    for k in range(groups - 1):
        j = order[k]
        remote(zbuf.at[j], zbuf.at[j], z_send.at[k], z_recv.at[j], (t, j)).wait_recv()
        crossings.append(send(zbuf.at[j], xbuf.at[k], x_send.at[k], x_recv.at[k], (column[1], g)))
        arrived = load(zbuf, j)
        for e in range(CORES, near):
            sbuf[k, e - CORES] = choose(arrived, e, j)
        for e in range(CORES, near):
            at = e - CORES
            picked[e // CORES].append(
                send(sbuf.at[k, at], abuf.at[k, at], a_send.at[k, at], a_recv.at[k, at], (column[e], g)))
    for k in range(groups - 1):
        crossings[k].wait_recv()
        j = order[k]
        own = add(own, term([choose(load(zbuf, j), 0, j), choose(load(xbuf, k), 0, j)], j))
    finish(0, own)
    for q in range(1, places):
        for r in range(CORES):
            blocks[q * CORES + r - 1].wait_recv()
        totals = term([choose(load(pbuf, q * CORES + r - 1), 0, g) for r in range(CORES)], g)
        for k in range(groups - 1):
            for r in range(CORES):
                picked[q][k * CORES + r].wait_recv()
            totals = add(totals, term([abuf[k, (q - 1) * CORES + r] for r in range(CORES)], order[k]))
        finish(q, totals)

    mine = jnp.int32(0)
    for q in range(places):
        mine = mine + q * (spot[q] == g).astype(jnp.int32)
    total = acc[mine]
    for k in range(groups - 1):
        j = order[k]
        remote(sums_buf.at[j], sums_buf.at[j], rs_send.at[0], rs_recv.at[j], (t, j)).wait_recv()
        total = total + sums_buf[j].astype(jnp.float32)
    total = (0.5 * total).astype(out_ref.dtype)
    half = total.shape[0] // CORES
    shape = (out_ref.shape[0], out_ref.shape[1] // CORES, out_ref.shape[2])
    same, other = total[:half].reshape(shape), total[half:].reshape(shape)
    first = core == 0
    out_ref[:, :shape[1], :] = jnp.where(first, same, other)
    out_ref[:, shape[1]:, :] = jnp.where(first, other, same)
    for copy in started:
        copy.wait_send()
    for q in range(places):
        @pl.when(spot[q] != g)
        def _():
            remote(rs_buf.at[q], sums_buf.at[g], rs_send.at[q], rs_recv.at[g], (t, spot[q])).wait_send()


def fused(groups, tiles, amplitudes, integrals, slot_cd, slot_ab):
    batch, pairs_dev, span = amplitudes.shape
    widths = integrals.shape[-1]
    places = tiles // CORES
    rows = pairs_dev * tiles // groups
    result = NT_DEV * widths
    tiles_dev = span // widths
    hbm = pl.BlockSpec(memory_space=pltpu.HBM)
    block = (tiles_dev, batch, pairs_dev, widths)
    piece = CORES * batch * pairs_dev
    others, around = groups - 1, CORES * (places - 1)
    dma = pltpu.SemaphoreType.DMA
    return pl.pallas_call(
        functools.partial(kernel, groups, places),
        out_shape=jax.ShapeDtypeStruct((batch, rows, result), jnp.bfloat16),
        in_specs=[hbm] * 4,
        out_specs=pl.BlockSpec(memory_space=pltpu.VMEM),
        scratch_shapes=[
            pltpu.VMEM((groups, *block), jnp.bfloat16),
            pltpu.VMEM((others, *block), jnp.bfloat16),
            pltpu.VMEM((tiles - 1, *block), jnp.bfloat16),
            pltpu.VMEM((others, around, batch, pairs_dev, widths), jnp.bfloat16),
            pltpu.VMEM((others, around, batch, pairs_dev, widths), jnp.bfloat16),
            pltpu.VMEM(integrals.shape, jnp.bfloat16),
            pltpu.VMEM((places, piece, result), jnp.float32),
            pltpu.VMEM((places, piece, result), jnp.bfloat16),
            pltpu.VMEM((groups, piece, result), jnp.bfloat16),
            pltpu.SMEM((tiles, *slot_cd.shape), jnp.int32),
            pltpu.SMEM(slot_ab.shape, jnp.int32),
            dma((tiles_dev,)),
            dma((3,)),
            dma((others,)),
            dma((groups,)),
            dma((tiles - 1,)),
            dma((tiles - 1,)),
            dma((tiles - 1,)),
            dma((tiles - 1,)),
            dma((others,)),
            dma((others,)),
            dma((others, around)),
            dma((others, around)),
            dma((places,)),
            dma((groups,)),
        ],
        compiler_params=pltpu.CompilerParams(collective_id=0, has_side_effects=True, vmem_limit_bytes=8 * 2**20),
    )(*(pltpu.with_memory_space_constraint(x, pltpu.HBM) for x in (amplitudes, integrals, slot_cd, slot_ab)))


def accumulate(slot_operands, slot_tiles, ab_list):
    row_count = slot_operands.shape[0]
    widths = slot_tiles.shape[-1]
    products = jnp.einsum(
        "rsc,scd->rsd", slot_operands, slot_tiles, preferred_element_type=jnp.float32
    )
    select = (ab_list[:, None] == jnp.arange(NT_DEV, dtype=jnp.int32)[None, :]).astype(jnp.float32)
    summed = jnp.einsum("rsd,sa->rad", products, select)
    return summed.reshape(row_count, NT_DEV * widths)


def by_slabs(amplitudes, integrals, slot_cd, slot_ab):
    groups = lax.axis_size("grp")
    own_index = lax.axis_index("grp")
    widths = integrals.shape[-1]
    pairs = amplitudes.shape[1] * lax.axis_size("tile")
    cd_table = slot_cd[0].reshape(groups, groups)
    ab_table = slot_ab[0].reshape(groups, groups)
    own_tiles = integrals[0]
    moved_tiles = lax.all_to_all(own_tiles, "grp", split_axis=0, concat_axis=0, tiled=True)
    cd_list = lax.dynamic_index_in_dim(cd_table, own_index, 1, keepdims=False)
    ab_list = lax.dynamic_index_in_dim(ab_table, own_index, 1, keepdims=False)
    outputs = []
    for batch_index in range(BATCH):
        slab_block = lax.all_gather(amplitudes[batch_index], "tile", axis=0, tiled=True)
        blocks = slab_block.reshape(pairs, slab_block.shape[1] // widths, widths)
        operands = jnp.take(blocks, cd_list, axis=1)
        full_terms = accumulate(operands, moved_tiles, ab_list)
        partial_value = lax.psum_scatter(full_terms, "grp", scatter_dimension=0, tiled=True)
        outputs.append((0.5 * partial_value).astype(jnp.bfloat16))
    return jnp.stack(outputs)


def solution(mesh):
    groups, tiles = mesh.shape["grp"], mesh.shape["tile"]

    def per_device(amplitudes, integrals, slot_cd, slot_ab):
        gathered = amplitudes.size * amplitudes.dtype.itemsize * groups * tiles
        if gathered > GATHER_LIMIT or tiles != CORES * groups or tiles & (tiles - 1):
            return by_slabs(amplitudes, integrals, slot_cd, slot_ab)
        return fused(groups, tiles, amplitudes, integrals, slot_cd, slot_ab)

    return jax.shard_map(
        per_device,
        mesh=mesh,
        in_specs=(
            P(None, "tile", "grp"),
            P("tile", "grp", None, None),
            P("tile", None),
            P("tile", None),
        ),
        out_specs=P(None, "grp", "tile"),
        check_vma=False,
    )
```

time: 21.9 us -> 18.7 us (0.85)
  the two profiles are of different devices: /device:TPU:0 before, /device:TPU:4 now
where the time goes in v1:
time: 18.7 us; the launch traced here: 18.5 us
  Pallas kernels  17.9 us (96%)
  local copies, waits for them, and re-layouts  0.62 us (3%)
    pallas_call x1, Pallas kernels, fused(): pl.pallas_call(functools.partial(kernel, groups, places), out_shape=jax.S...  17.9 us
    unnamed x1, local copies, waits for them, and re-layouts  0.62 us

profile of v1, /device:TPU:4, one launch (start us, length us, event | category | flops | bytes accessed | tf_op | source)
XLA Modules:
  0.0 18.5 jit_solution(6691370940280965745)
XLA Ops:
  0.0 17.9 %shard_map.46 = bf16[2,16,512]{2,1,0:T(8,128)(2,1)S(1)} custom-call(bf16[2,8,1024]{2,1,0:T(8,128)(2,1)} %amp_ref.1, bf16[1,4,256,256]{3,2,1,0:T(8,128)(2,1)} %int_ref.1, s32[1,16]{1,0:T(1,128)} %cd_ref.1, s32[1,16]{1,0:T(1,128)} %ab_ref.1), custom_call_target="tpu_custom_call" | custom-call | tf_op jit(solution)/shard_map/pallas_call | solution.py:183
  17.9 0.6 %copy.6 = bf16[2,16,512]{2,1,0:T(8,128)(2,1)} copy(bf16[2,16,512]{2,1,0:T(8,128)(2,1)S(1)} %shard_map.46) | data formatting | bytes 65536

commit v2 on v1

v2 whole, which is shorter than its diff:
```python
import functools

import jax
import jax.numpy as jnp
from jax import lax
from jax.experimental import pallas as pl
from jax.experimental.pallas import tpu as pltpu
from jax.sharding import PartitionSpec as P

MESH = pl.DeviceIdType.MESH
NT_DEV = 2
BATCH = 2
GATHER_LIMIT = 8 * 2**20
CORES = 2


def farthest_first(own, count):
    low, high = jnp.int32(0), jnp.int32(count - 1)
    order = []
    for _ in range(count - 1):
        take_low = (own - low >= high - own).astype(jnp.int32)
        order.append(take_low * low + (1 - take_low) * high)
        low, high = low + take_low, high - (1 - take_low)
    return order


def kernel(groups, places, amp_ref, int_ref, cd_ref, ab_ref, out_ref, zbuf, xbuf, pbuf, abuf, sbuf, tile_buf, acc, rs_buf,
           sums_buf, cd_smem, ab_smem, local_sem, z_send, z_recv, t_send, t_recv, p_send, p_recv, x_send, x_recv,
           a_send, a_recv, rs_send, rs_recv):
    g, t = lax.axis_index("grp"), lax.axis_index("tile")
    place, core = lax.div(t, jnp.int32(CORES)), lax.rem(t, jnp.int32(CORES))
    widths = int_ref.shape[-1]
    tiles_dev = zbuf.shape[1]
    partner = place * CORES + 1 - core
    rest = [i + (i >= place).astype(jnp.int32) for i in range(places - 1)]
    around = [where * CORES + c for where in rest for c in range(CORES)]
    order = farthest_first(g, groups)
    nearest = order[::-1]
    piece = acc.shape[1]

    barrier = pltpu.get_barrier_semaphore()
    peers = [(t, z) for z in order] + [(column, g) for column in (partner, *around)]
    for peer in peers:
        pl.semaphore_signal(barrier, inc=1, device_id=peer, device_id_type=MESH)
    amp_copies = [
        pltpu.make_async_copy(amp_ref.at[:, :, pl.ds(c * widths, widths)], zbuf.at[g, c], local_sem.at[3])
        for c in range(tiles_dev)
    ]
    cd_copy = pltpu.make_async_copy(cd_ref, cd_smem.at[t], local_sem.at[0])
    ab_copy = pltpu.make_async_copy(ab_ref, ab_smem, local_sem.at[1])
    int_copy = pltpu.make_async_copy(int_ref, tile_buf, local_sem.at[2])
    for copy in (cd_copy, *amp_copies, ab_copy, int_copy):
        copy.start()
    pl.semaphore_wait(barrier, len(peers))

    def remote(src, dst, send, recv, peer):
        return pltpu.make_async_remote_copy(
            src_ref=src, dst_ref=dst, send_sem=send, recv_sem=recv, device_id=peer, device_id_type=MESH)

    def send(*what):
        remote(*what).start()

    def arrived(dst, recv):
        remote(dst, dst, z_send, recv, (t, z_first)).wait_recv()

    def left(src, sem):
        remote(src, src, sem, t_recv, (t, z_first)).wait_send()

    z_first = order[0]
    cd_copy.wait()
    for column in around:
        send(cd_smem.at[t], cd_smem.at[t], t_send, t_recv, (column, g))
    pltpu.make_async_copy(zbuf.at[g], zbuf.at[g], local_sem.at[3]).wait()
    for z in order:
        send(zbuf.at[g], zbuf.at[g], z_send, z_recv.at[g], (t, z))
    send(zbuf.at[g], pbuf.at[t], p_send, p_recv.at[0], (partner, g))
    for column in around:
        send(zbuf.at[g], pbuf.at[t], p_send, p_recv.at[1], (column, g))
    ab_copy.wait()
    int_copy.wait()

    def load(buf, at):
        return [buf[at, c] for c in range(tiles_dev)]

    def choose(tiles, column, j):
        cd = cd_smem[column, 0, g * groups + j]
        chosen = tiles[0]
        for c in range(1, tiles_dev):
            chosen = jnp.where(cd == c, tiles[c], chosen)
        return chosen

    def term(parts, j):
        operand = jnp.concatenate([part.reshape(-1, widths) for part in parts], axis=0)
        product = jnp.dot(operand, tile_buf[0, j], preferred_element_type=jnp.float32)
        ab = ab_smem[0, g * groups + j]
        return [product * (ab == a).astype(jnp.float32) for a in range(NT_DEV)]

    def add(left, right):
        return [x + y for x, y in zip(left, right)]

    def finish(where, totals):
        for a in range(NT_DEV):
            acc[where, :, a * widths:(a + 1) * widths] = totals[a]
            rs_buf[where, :, a * widths:(a + 1) * widths] = totals[a].astype(rs_buf.dtype)

        @pl.when(where != g)
        def _():
            send(rs_buf.at[where], sums_buf.at[g], rs_send, rs_recv, (t, where))

    arrived(pbuf.at[partner], p_recv.at[0])
    own = term([choose(load(zbuf, g), t, g), choose(load(pbuf, partner), t, g)], g)
    arrived(cd_smem.at[pl.ds(0, len(around))], t_recv)
    for k, j in enumerate(nearest):
        arrived(zbuf.at[j], z_recv.at[j])
        send(zbuf.at[j], xbuf.at[k], x_send, x_recv, (partner, g))
        tiles = load(zbuf, j)
        for e, column in enumerate(around):
            sbuf[k, e] = choose(tiles, column, j)
        for e, column in enumerate(around):
            send(sbuf.at[k, e], abuf.at[k, t], a_send, a_recv.at[k], (column, g))
    arrived(xbuf, x_recv)
    for k, j in enumerate(nearest):
        own = add(own, term([choose(load(zbuf, j), t, j), choose(load(xbuf, k), t, j)], j))
    finish(place, own)

    columns = [[where * CORES + (1 - core if r else core) for r in range(CORES)] for where in rest]
    operands = []
    arrived(pbuf.at[pl.ds(0, len(around))], p_recv.at[1])
    for pair in columns:
        for column in pair:
            operands.append(choose(load(pbuf, column), t, g))
    sums = term(operands, g)

    for k, j in enumerate(nearest):
        arrived(abuf.at[k, pl.ds(0, len(around))], a_recv.at[k])
        sums = add(sums, term([abuf[k, column] for pair in columns for column in pair], j))
    for at, where in enumerate(rest):
        finish(where, [x[at * piece:(at + 1) * piece] for x in sums])

    total = acc[g]
    arrived(sums_buf.at[pl.ds(0, groups - 1)], rs_recv)
    for j in nearest:
        total = total + sums_buf[j].astype(jnp.float32)
    total = (0.5 * total).astype(out_ref.dtype)
    half = total.shape[0] // CORES
    shape = (out_ref.shape[0], out_ref.shape[1] // CORES, out_ref.shape[2])
    same, other = total[:half].reshape(shape), total[half:].reshape(shape)
    first = core == 0
    out_ref[:, :shape[1], :] = jnp.where(first, same, other)
    out_ref[:, shape[1]:, :] = jnp.where(first, other, same)
    left(cd_smem.at[pl.ds(0, len(around))], t_send)
    left(zbuf.at[pl.ds(0, groups - 1)], z_send)
    left(pbuf.at[pl.ds(0, len(around) + 1)], p_send)
    left(xbuf, x_send)
    left(sbuf, a_send)
    left(rs_buf.at[pl.ds(0, groups - 1)], rs_send)


def fused(groups, tiles, amplitudes, integrals, slot_cd, slot_ab):
    batch, pairs_dev, span = amplitudes.shape
    widths = integrals.shape[-1]
    places = tiles // CORES
    rows = pairs_dev * tiles // groups
    result = NT_DEV * widths
    tiles_dev = span // widths
    hbm = pl.BlockSpec(memory_space=pltpu.HBM)
    block = (tiles_dev, batch, pairs_dev, widths)
    piece = CORES * batch * pairs_dev
    others, around = groups - 1, CORES * (places - 1)
    dma = pltpu.SemaphoreType.DMA
    return pl.pallas_call(
        functools.partial(kernel, groups, places),
        out_shape=jax.ShapeDtypeStruct((batch, rows, result), jnp.bfloat16),
        in_specs=[hbm] * 4,
        out_specs=pl.BlockSpec(memory_space=pltpu.VMEM),
        scratch_shapes=[
            pltpu.VMEM((groups, *block), jnp.bfloat16),
            pltpu.VMEM((others, *block), jnp.bfloat16),
            pltpu.VMEM((tiles, *block), jnp.bfloat16),
            pltpu.VMEM((others, tiles, batch, pairs_dev, widths), jnp.bfloat16),
            pltpu.VMEM((others, around, batch, pairs_dev, widths), jnp.bfloat16),
            pltpu.VMEM(integrals.shape, jnp.bfloat16),
            pltpu.VMEM((places, piece, result), jnp.float32),
            pltpu.VMEM((places, piece, result), jnp.bfloat16),
            pltpu.VMEM((groups, piece, result), jnp.bfloat16),
            pltpu.SMEM((tiles, *slot_cd.shape), jnp.int32),
            pltpu.SMEM(slot_ab.shape, jnp.int32),
            dma((4,)),
            dma,
            dma((groups,)),
            dma,
            dma,
            dma,
            dma((2,)),
            dma,
            dma,
            dma,
            dma((others,)),
            dma,
            dma,
        ],
        compiler_params=pltpu.CompilerParams(collective_id=0, has_side_effects=True, vmem_limit_bytes=8 * 2**20),
    )(*(pltpu.with_memory_space_constraint(x, pltpu.HBM) for x in (amplitudes, integrals, slot_cd, slot_ab)))


def accumulate(slot_operands, slot_tiles, ab_list):
    row_count = slot_operands.shape[0]
    widths = slot_tiles.shape[-1]
    products = jnp.einsum(
        "rsc,scd->rsd", slot_operands, slot_tiles, preferred_element_type=jnp.float32
    )
    select = (ab_list[:, None] == jnp.arange(NT_DEV, dtype=jnp.int32)[None, :]).astype(jnp.float32)
    summed = jnp.einsum("rsd,sa->rad", products, select)
    return summed.reshape(row_count, NT_DEV * widths)


def by_slabs(amplitudes, integrals, slot_cd, slot_ab):
    groups = lax.axis_size("grp")
    own_index = lax.axis_index("grp")
    widths = integrals.shape[-1]
    pairs = amplitudes.shape[1] * lax.axis_size("tile")
    cd_table = slot_cd[0].reshape(groups, groups)
    ab_table = slot_ab[0].reshape(groups, groups)
    own_tiles = integrals[0]
    moved_tiles = lax.all_to_all(own_tiles, "grp", split_axis=0, concat_axis=0, tiled=True)
    cd_list = lax.dynamic_index_in_dim(cd_table, own_index, 1, keepdims=False)
    ab_list = lax.dynamic_index_in_dim(ab_table, own_index, 1, keepdims=False)
    outputs = []
    for batch_index in range(BATCH):
        slab_block = lax.all_gather(amplitudes[batch_index], "tile", axis=0, tiled=True)
        blocks = slab_block.reshape(pairs, slab_block.shape[1] // widths, widths)
        operands = jnp.take(blocks, cd_list, axis=1)
        full_terms = accumulate(operands, moved_tiles, ab_list)
        partial_value = lax.psum_scatter(full_terms, "grp", scatter_dimension=0, tiled=True)
        outputs.append((0.5 * partial_value).astype(jnp.bfloat16))
    return jnp.stack(outputs)


def solution(mesh):
    groups, tiles = mesh.shape["grp"], mesh.shape["tile"]

    def per_device(amplitudes, integrals, slot_cd, slot_ab):
        gathered = amplitudes.size * amplitudes.dtype.itemsize * groups * tiles
        if gathered > GATHER_LIMIT or tiles != CORES * groups or tiles & (tiles - 1):
            return by_slabs(amplitudes, integrals, slot_cd, slot_ab)
        return fused(groups, tiles, amplitudes, integrals, slot_cd, slot_ab)

    return jax.shard_map(
        per_device,
        mesh=mesh,
        in_specs=(
            P(None, "tile", "grp"),
            P("tile", "grp", None, None),
            P("tile", None),
            P("tile", None),
        ),
        out_specs=P(None, "grp", "tile"),
        check_vma=False,
    )
```

time: 18.7 us -> 17.2 us (0.920)
  the two profiles are of different devices: /device:TPU:4 before, /device:TPU:5 now
where the time goes in v2:
time: 17.2 us; the launch traced here: 17.1 us
  Pallas kernels  16.4 us (95%)
  local copies, waits for them, and re-layouts  0.62 us (4%)
    pallas_call x1, Pallas kernels, fused(): pl.pallas_call(functools.partial(kernel, groups, places), out_shape=jax.S...  16.4 us
    unnamed x1, local copies, waits for them, and re-layouts  0.62 us

profile of v2, /device:TPU:5, one launch (start us, length us, event | category | flops | bytes accessed | tf_op | source)
XLA Modules:
  0.0 17.1 jit_solution(16101380604605907991)
XLA Ops:
  0.0 16.4 %shard_map.46 = bf16[2,16,512]{2,1,0:T(8,128)(2,1)S(1)} custom-call(bf16[2,8,1024]{2,1,0:T(8,128)(2,1)} %amp_ref.1, bf16[1,4,256,256]{3,2,1,0:T(8,128)(2,1)} %int_ref.1, s32[1,16]{1,0:T(1,128)} %cd_ref.1, s32[1,16]{1,0:T(1,128)} %ab_ref.1), custom_call_target="tpu_custom_call" | custom-call | tf_op jit(solution)/shard_map/pallas_call | solution.py:171
  16.4 0.6 %copy.6 = bf16[2,16,512]{2,1,0:T(8,128)(2,1)} copy(bf16[2,16,512]{2,1,0:T(8,128)(2,1)S(1)} %shard_map.46) | data formatting | bytes 65536

commit v3 on v2

v3 whole, which is shorter than its diff:
```python
import functools

import jax
import jax.numpy as jnp
from jax import lax
from jax.experimental import pallas as pl
from jax.experimental.pallas import tpu as pltpu
from jax.sharding import PartitionSpec as P

MESH = pl.DeviceIdType.MESH
NT_DEV = 2
BATCH = 2
GATHER_LIMIT = 8 * 2**20
CORES = 2


def farthest_first(own, count):
    low, high = jnp.int32(0), jnp.int32(count - 1)
    order = []
    for _ in range(count - 1):
        take_low = (own - low >= high - own).astype(jnp.int32)
        order.append(take_low * low + (1 - take_low) * high)
        low, high = low + take_low, high - (1 - take_low)
    return order


def flip(index, mask):
    bit = 1
    while bit <= mask:
        if mask & bit:
            index = index + bit * (1 - 2 * lax.rem(lax.div(index, jnp.int32(bit)), jnp.int32(2)))
        bit *= 2
    return index


def kernel(groups, places, amp_ref, int_ref, cd_ref, ab_ref, out_ref, zbuf, xbuf, pbuf, abuf, sbuf, tile_buf, acc, rs_buf,
           sums_buf, cd_smem, ab_smem, local_sem, z_send, z_recv, t_send, t_recv, p_send, p_recv, x_send, x_recv,
           a_send, a_recv, rs_send, rs_recv):
    g, t = lax.axis_index("grp"), lax.axis_index("tile")
    place, core = lax.div(t, jnp.int32(CORES)), lax.rem(t, jnp.int32(CORES))
    widths = int_ref.shape[-1]
    _, batch, tiles_dev, pairs_dev, _ = zbuf.shape
    piece = CORES * pairs_dev
    partner = place * CORES + 1 - core
    rest = [flip(place, q) for q in (*range(places // 2, places), *range(1, places // 2))]
    around = [where * CORES + c for where in rest for c in range(CORES)]
    columns = [[where * CORES + (1 - core if r else core) for r in range(CORES)] for where in rest]
    order = farthest_first(g, groups)
    nearest = order[::-1]

    barrier = pltpu.get_barrier_semaphore()
    peers = [(t, z) for z in order] + [(column, g) for column in (partner, *around)]
    for peer in peers:
        pl.semaphore_signal(barrier, inc=1, device_id=peer, device_id_type=MESH)
    cd_copy = pltpu.make_async_copy(cd_ref, cd_smem.at[t], local_sem.at[0])
    ab_copy = pltpu.make_async_copy(ab_ref, ab_smem, local_sem.at[1])
    int_copy = pltpu.make_async_copy(int_ref, tile_buf, local_sem.at[2])
    cd_copy.start()
    for h in range(batch):
        for c in range(tiles_dev):
            pltpu.make_async_copy(amp_ref.at[h, :, pl.ds(c * widths, widths)], zbuf.at[g, h, c], local_sem.at[3]).start()
    ab_copy.start()
    int_copy.start()
    pl.semaphore_wait(barrier, len(peers))

    def send(src, dst, sent, recv, peer):
        pltpu.make_async_remote_copy(
            src_ref=src, dst_ref=dst, send_sem=sent, recv_sem=recv, device_id=peer, device_id_type=MESH).start()

    def arrived(dst, recv):
        pltpu.make_async_remote_copy(
            src_ref=dst, dst_ref=dst, send_sem=z_send, recv_sem=recv, device_id=peers[0], device_id_type=MESH).wait_recv()

    def left(src, sent):
        pltpu.make_async_remote_copy(
            src_ref=src, dst_ref=src, send_sem=sent, recv_sem=t_recv, device_id=peers[0], device_id_type=MESH).wait_send()

    cd_copy.wait()
    for column in around:
        send(cd_smem.at[t], cd_smem.at[t], t_send, t_recv, (column, g))
    pltpu.make_async_copy(zbuf.at[g], zbuf.at[g], local_sem.at[3]).wait()
    for h in range(batch):
        for z in order[::-1]:
            send(zbuf.at[g, h], zbuf.at[g, h], z_send, z_recv.at[g, h], (t, z))
    send(zbuf.at[g], pbuf.at[t], p_send, p_recv.at[0], (partner, g))
    for column in around:
        send(zbuf.at[g], pbuf.at[t], p_send, p_recv.at[1], (column, g))
    ab_copy.wait()
    int_copy.wait()

    def load(*at):
        buf, *at = at
        return [buf[(*at, c)] for c in range(tiles_dev)]

    def choose(tiles, column, j):
        cd = cd_smem[column, 0, g * groups + j]
        chosen = tiles[0]
        for c in range(1, tiles_dev):
            chosen = jnp.where(cd == c, tiles[c], chosen)
        return chosen

    def term(parts, j):
        operand = jnp.concatenate(parts, axis=0)
        product = jnp.dot(operand, tile_buf[0, j], preferred_element_type=jnp.float32)
        ab = ab_smem[0, g * groups + j]
        return [product * (ab == a).astype(jnp.float32) for a in range(NT_DEV)]

    def add(left, right):
        return [x + y for x, y in zip(left, right)]

    def finish(h, where, totals):
        for a in range(NT_DEV):
            acc[h, where, :, a * widths:(a + 1) * widths] = totals[a]
            rs_buf[h, where, :, a * widths:(a + 1) * widths] = totals[a].astype(rs_buf.dtype)

        @pl.when(where != g)
        def _():
            send(rs_buf.at[h, where], sums_buf.at[h, g], rs_send, rs_recv.at[h], (t, where))

    halves = range(batch)
    arrived(pbuf.at[partner], p_recv.at[0])
    own = [part for h in halves for part in (choose(load(zbuf, g, h), t, g), choose(load(pbuf, partner, h), t, g))]
    own = term(own, g)
    arrived(cd_smem.at[pl.ds(0, len(around))], t_recv)
    for h in halves:
        for k, j in enumerate(nearest):
            arrived(zbuf.at[j, h], z_recv.at[j, h])
            send(zbuf.at[j, h], xbuf.at[k, h], x_send, x_recv, (partner, g))
            tiles = load(zbuf, j, h)
            for e, column in enumerate(around):
                sbuf[h, k, e] = choose(tiles, column, j)
            for e, column in enumerate(around):
                send(sbuf.at[h, k, e], abuf.at[h, k, t], a_send, a_recv.at[h, k], (column, g))
    arrived(xbuf, x_recv)
    for k, j in enumerate(nearest):
        parts = [part for h in halves for part in (choose(load(zbuf, j, h), t, j), choose(load(xbuf, k, h), t, j))]
        own = add(own, term(parts, j))
    for h in halves:
        finish(h, place, [x[h * piece:(h + 1) * piece] for x in own])

    arrived(pbuf.at[pl.ds(0, len(around))], p_recv.at[1])
    parts = [choose(load(pbuf, column, h), t, g) for h in halves for pair in columns for column in pair]
    base = term(parts, g)
    rows = piece * len(rest)
    for h in halves:
        sums = [x[h * rows:(h + 1) * rows] for x in base]
        for k, j in enumerate(nearest):
            arrived(abuf.at[h, k, pl.ds(0, len(around))], a_recv.at[h, k])
            sums = add(sums, term([abuf[h, k, column] for pair in columns for column in pair], j))
        for at, where in enumerate(rest):
            finish(h, where, [x[at * piece:(at + 1) * piece] for x in sums])

    first = core == 0
    for h in halves:
        total = acc[h, g]
        arrived(sums_buf.at[h, pl.ds(0, groups - 1)], rs_recv.at[h])
        for j in nearest:
            total = total + sums_buf[h, j].astype(jnp.float32)
        total = (0.5 * total).astype(out_ref.dtype)
        same, other = total[:pairs_dev], total[pairs_dev:]
        out_ref[h, :pairs_dev, :] = jnp.where(first, same, other)
        out_ref[h, pairs_dev:, :] = jnp.where(first, other, same)
    left(cd_smem.at[pl.ds(0, len(around))], t_send)
    left(zbuf.at[pl.ds(0, groups - 1)], z_send)
    left(pbuf.at[pl.ds(0, len(around) + 1)], p_send)
    left(xbuf, x_send)
    left(sbuf, a_send)
    left(rs_buf.at[:, pl.ds(0, groups - 1)], rs_send)


def fused(groups, tiles, amplitudes, integrals, slot_cd, slot_ab):
    batch, pairs_dev, span = amplitudes.shape
    widths = integrals.shape[-1]
    places = tiles // CORES
    rows = pairs_dev * tiles // groups
    result = NT_DEV * widths
    tiles_dev = span // widths
    hbm = pl.BlockSpec(memory_space=pltpu.HBM)
    block = (batch, tiles_dev, pairs_dev, widths)
    piece = CORES * pairs_dev
    others, around = groups - 1, CORES * (places - 1)
    dma = pltpu.SemaphoreType.DMA
    return pl.pallas_call(
        functools.partial(kernel, groups, places),
        out_shape=jax.ShapeDtypeStruct((batch, rows, result), jnp.bfloat16),
        in_specs=[hbm] * 4,
        out_specs=pl.BlockSpec(memory_space=pltpu.VMEM),
        scratch_shapes=[
            pltpu.VMEM((groups, *block), jnp.bfloat16),
            pltpu.VMEM((others, *block), jnp.bfloat16),
            pltpu.VMEM((tiles, *block), jnp.bfloat16),
            pltpu.VMEM((batch, others, tiles, pairs_dev, widths), jnp.bfloat16),
            pltpu.VMEM((batch, others, around, pairs_dev, widths), jnp.bfloat16),
            pltpu.VMEM(integrals.shape, jnp.bfloat16),
            pltpu.VMEM((batch, places, piece, result), jnp.float32),
            pltpu.VMEM((batch, places, piece, result), jnp.bfloat16),
            pltpu.VMEM((batch, groups, piece, result), jnp.bfloat16),
            pltpu.SMEM((tiles, *slot_cd.shape), jnp.int32),
            pltpu.SMEM(slot_ab.shape, jnp.int32),
            dma((4,)),
            dma,
            dma((groups, batch)),
            dma,
            dma,
            dma,
            dma((2,)),
            dma,
            dma,
            dma,
            dma((batch, others)),
            dma,
            dma((batch,)),
        ],
        compiler_params=pltpu.CompilerParams(collective_id=0, has_side_effects=True, vmem_limit_bytes=8 * 2**20),
    )(*(pltpu.with_memory_space_constraint(x, pltpu.HBM) for x in (amplitudes, integrals, slot_cd, slot_ab)))


def accumulate(slot_operands, slot_tiles, ab_list):
    row_count = slot_operands.shape[0]
    widths = slot_tiles.shape[-1]
    products = jnp.einsum(
        "rsc,scd->rsd", slot_operands, slot_tiles, preferred_element_type=jnp.float32
    )
    select = (ab_list[:, None] == jnp.arange(NT_DEV, dtype=jnp.int32)[None, :]).astype(jnp.float32)
    summed = jnp.einsum("rsd,sa->rad", products, select)
    return summed.reshape(row_count, NT_DEV * widths)


def by_slabs(amplitudes, integrals, slot_cd, slot_ab):
    groups = lax.axis_size("grp")
    own_index = lax.axis_index("grp")
    widths = integrals.shape[-1]
    pairs = amplitudes.shape[1] * lax.axis_size("tile")
    cd_table = slot_cd[0].reshape(groups, groups)
    ab_table = slot_ab[0].reshape(groups, groups)
    own_tiles = integrals[0]
    moved_tiles = lax.all_to_all(own_tiles, "grp", split_axis=0, concat_axis=0, tiled=True)
    cd_list = lax.dynamic_index_in_dim(cd_table, own_index, 1, keepdims=False)
    ab_list = lax.dynamic_index_in_dim(ab_table, own_index, 1, keepdims=False)
    outputs = []
    for batch_index in range(BATCH):
        slab_block = lax.all_gather(amplitudes[batch_index], "tile", axis=0, tiled=True)
        blocks = slab_block.reshape(pairs, slab_block.shape[1] // widths, widths)
        operands = jnp.take(blocks, cd_list, axis=1)
        full_terms = accumulate(operands, moved_tiles, ab_list)
        partial_value = lax.psum_scatter(full_terms, "grp", scatter_dimension=0, tiled=True)
        outputs.append((0.5 * partial_value).astype(jnp.bfloat16))
    return jnp.stack(outputs)


def solution(mesh):
    groups, tiles = mesh.shape["grp"], mesh.shape["tile"]

    def per_device(amplitudes, integrals, slot_cd, slot_ab):
        gathered = amplitudes.size * amplitudes.dtype.itemsize * groups * tiles
        if gathered > GATHER_LIMIT or tiles != CORES * groups or tiles & (tiles - 1):
            return by_slabs(amplitudes, integrals, slot_cd, slot_ab)
        return fused(groups, tiles, amplitudes, integrals, slot_cd, slot_ab)

    return jax.shard_map(
        per_device,
        mesh=mesh,
        in_specs=(
            P(None, "tile", "grp"),
            P("tile", "grp", None, None),
            P("tile", None),
            P("tile", None),
        ),
        out_specs=P(None, "grp", "tile"),
        check_vma=False,
    )
```

time: 17.2 us -> 16.7 us (0.971)
  the two profiles are of different devices: /device:TPU:5 before, /device:TPU:4 now
where the time goes in v3:
time: 16.7 us; the launch traced here: 16.5 us
  Pallas kernels  15.9 us (95%)
  local copies, waits for them, and re-layouts  0.62 us (4%)
    pallas_call x1, Pallas kernels, fused(): pl.pallas_call(functools.partial(kernel, groups, places), out_shape=jax.S...  15.9 us
    unnamed x1, local copies, waits for them, and re-layouts  0.62 us

profile of v3, /device:TPU:4, one launch (start us, length us, event | category | flops | bytes accessed | tf_op | source)
XLA Modules:
  0.0 16.5 jit_solution(10494683187132705336)
XLA Ops:
  0.0 15.9 %shard_map.46 = bf16[2,16,512]{2,1,0:T(8,128)(2,1)S(1)} custom-call(bf16[2,8,1024]{2,1,0:T(8,128)(2,1)} %amp_ref.1, bf16[1,4,256,256]{3,2,1,0:T(8,128)(2,1)} %int_ref.1, s32[1,16]{1,0:T(1,128)} %cd_ref.1, s32[1,16]{1,0:T(1,128)} %ab_ref.1), custom_call_target="tpu_custom_call" | custom-call | tf_op jit(solution)/shard_map/pallas_call | solution.py:183
  15.9 0.6 %copy.6 = bf16[2,16,512]{2,1,0:T(8,128)(2,1)} copy(bf16[2,16,512]{2,1,0:T(8,128)(2,1)S(1)} %shard_map.46) | data formatting | bytes 65536

commit v4 on v3

--- a/solution.py
+++ b/solution.py
@@ -44,7 +44,8 @@
     partner = place * CORES + 1 - core
     rest = [flip(place, q) for q in (*range(places // 2, places), *range(1, places // 2))]
     around = [where * CORES + c for where in rest for c in range(CORES)]
-    columns = [[where * CORES + (1 - core if r else core) for r in range(CORES)] for where in rest]
+    rising = [i + (i >= place).astype(jnp.int32) for i in range(places - 1)]
+    columns = [[where * CORES + (1 - core if r else core) for r in range(CORES)] for where in rising]
     order = farthest_first(g, groups)
     nearest = order[::-1]
 
@@ -130,7 +131,7 @@
             for e, column in enumerate(around):
                 sbuf[h, k, e] = choose(tiles, column, j)
             for e, column in enumerate(around):
-                send(sbuf.at[h, k, e], abuf.at[h, k, t], a_send, a_recv.at[h, k], (column, g))
+                send(sbuf.at[h, k, e], abuf.at[h, k, t], a_send, a_recv.at[h, place], (column, g))
     arrived(xbuf, x_recv)
     for k, j in enumerate(nearest):
         parts = [part for h in halves for part in (choose(load(zbuf, j, h), t, j), choose(load(xbuf, k, h), t, j))]
@@ -141,14 +142,14 @@
     arrived(pbuf.at[pl.ds(0, len(around))], p_recv.at[1])
     parts = [choose(load(pbuf, column, h), t, g) for h in halves for pair in columns for column in pair]
     base = term(parts, g)
-    rows = piece * len(rest)
-    for h in halves:
-        sums = [x[h * rows:(h + 1) * rows] for x in base]
+    for h, at in ((h, at) for h in halves for at in range(places - 1)):
+        where, pair = rising[at], columns[at]
+        start = (h * len(rising) + at) * piece
+        sums = [x[start:start + piece] for x in base]
+        arrived(abuf.at[h, :, pl.ds(0, CORES)], a_recv.at[h, where])
         for k, j in enumerate(nearest):
-            arrived(abuf.at[h, k, pl.ds(0, len(around))], a_recv.at[h, k])
-            sums = add(sums, term([abuf[h, k, column] for pair in columns for column in pair], j))
-        for at, where in enumerate(rest):
-            finish(h, where, [x[at * piece:(at + 1) * piece] for x in sums])
+            sums = add(sums, term([abuf[h, k, column] for column in pair], j))
+        finish(h, where, sums)
 
     first = core == 0
     for h in halves:
@@ -207,7 +208,7 @@
             dma,
             dma,
             dma,
-            dma((batch, others)),
+            dma((batch, places)),
             dma,
             dma((batch,)),
         ],

time: 16.7 us -> 16.3 us (0.976)
  the two profiles are of different devices: /device:TPU:4 before, /device:TPU:0 now
where the time goes in v4:
time: 16.3 us; the launch traced here: 16.2 us
  Pallas kernels  15.5 us (95%)
  local copies, waits for them, and re-layouts  0.62 us (4%)
    pallas_call x1, Pallas kernels, fused(): pl.pallas_call(functools.partial(kernel, groups, places), out_shape=jax.S...  15.5 us
    unnamed x1, local copies, waits for them, and re-layouts  0.62 us

profile of v4, /device:TPU:0, one launch (start us, length us, event | category | flops | bytes accessed | tf_op | source)
XLA Modules:
  0.0 16.2 jit_solution(210202981415877653)
XLA Ops:
  0.0 15.5 %shard_map.46 = bf16[2,16,512]{2,1,0:T(8,128)(2,1)S(1)} custom-call(bf16[2,8,1024]{2,1,0:T(8,128)(2,1)} %amp_ref.1, bf16[1,4,256,256]{3,2,1,0:T(8,128)(2,1)} %int_ref.1, s32[1,16]{1,0:T(1,128)} %cd_ref.1, s32[1,16]{1,0:T(1,128)} %ab_ref.1), custom_call_target="tpu_custom_call" | custom-call | tf_op jit(solution)/shard_map/pallas_call | solution.py:184
  15.6 0.6 %copy.6 = bf16[2,16,512]{2,1,0:T(8,128)(2,1)} copy(bf16[2,16,512]{2,1,0:T(8,128)(2,1)S(1)} %shard_map.46) | data formatting | bytes 65536

commit v5 on v4

--- a/solution.py
+++ b/solution.py
@@ -24,25 +24,19 @@
     return order
 
 
-def flip(index, mask):
-    bit = 1
-    while bit <= mask:
-        if mask & bit:
-            index = index + bit * (1 - 2 * lax.rem(lax.div(index, jnp.int32(bit)), jnp.int32(2)))
-        bit *= 2
-    return index
+def without(index, absent):
+    return index - (index > absent).astype(jnp.int32)
 
 
 def kernel(groups, places, amp_ref, int_ref, cd_ref, ab_ref, out_ref, zbuf, xbuf, pbuf, abuf, sbuf, tile_buf, acc, rs_buf,
-           sums_buf, cd_smem, ab_smem, local_sem, z_send, z_recv, t_send, t_recv, p_send, p_recv, x_send, x_recv,
-           a_send, a_recv, rs_send, rs_recv):
+           sums_buf, all_sent, tables, local_sem, sent, z_recv, t_send, t_recv, p_recv, x_recv, a_recv, rs_recv):
     g, t = lax.axis_index("grp"), lax.axis_index("tile")
     place, core = lax.div(t, jnp.int32(CORES)), lax.rem(t, jnp.int32(CORES))
     widths = int_ref.shape[-1]
     _, batch, tiles_dev, pairs_dev, _ = zbuf.shape
     piece = CORES * pairs_dev
     partner = place * CORES + 1 - core
-    rest = [flip(place, q) for q in (*range(places // 2, places), *range(1, places // 2))]
+    rest = [i + (i >= place).astype(jnp.int32) for i in range(places - 1)]
     around = [where * CORES + c for where in rest for c in range(CORES)]
     rising = [i + (i >= place).astype(jnp.int32) for i in range(places - 1)]
     columns = [[where * CORES + (1 - core if r else core) for r in range(CORES)] for where in rising]
@@ -53,40 +47,40 @@
     peers = [(t, z) for z in order] + [(column, g) for column in (partner, *around)]
     for peer in peers:
         pl.semaphore_signal(barrier, inc=1, device_id=peer, device_id_type=MESH)
-    cd_copy = pltpu.make_async_copy(cd_ref, cd_smem.at[t], local_sem.at[0])
-    ab_copy = pltpu.make_async_copy(ab_ref, ab_smem, local_sem.at[1])
-    int_copy = pltpu.make_async_copy(int_ref, tile_buf, local_sem.at[2])
+    near = places * CORES
+    cd_copy = pltpu.make_async_copy(cd_ref, tables.at[t], local_sem.at[0])
+    ab_copy = pltpu.make_async_copy(ab_ref, tables.at[near], local_sem.at[0])
+    int_copy = pltpu.make_async_copy(int_ref, tile_buf, local_sem.at[1])
     cd_copy.start()
+    ab_copy.start()
     for h in range(batch):
         for c in range(tiles_dev):
-            pltpu.make_async_copy(amp_ref.at[h, :, pl.ds(c * widths, widths)], zbuf.at[g, h, c], local_sem.at[3]).start()
-    ab_copy.start()
+            pltpu.make_async_copy(amp_ref.at[h, :, pl.ds(c * widths, widths)], zbuf.at[g, h, c], local_sem.at[2]).start()
     int_copy.start()
     pl.semaphore_wait(barrier, len(peers))
 
-    def send(src, dst, sent, recv, peer):
+    def send(src, dst, gone, recv, peer):
         pltpu.make_async_remote_copy(
-            src_ref=src, dst_ref=dst, send_sem=sent, recv_sem=recv, device_id=peer, device_id_type=MESH).start()
+            src_ref=src, dst_ref=dst, send_sem=gone, recv_sem=recv, device_id=peer, device_id_type=MESH).start()
 
     def arrived(dst, recv):
         pltpu.make_async_remote_copy(
-            src_ref=dst, dst_ref=dst, send_sem=z_send, recv_sem=recv, device_id=peers[0], device_id_type=MESH).wait_recv()
-
-    def left(src, sent):
+            src_ref=dst, dst_ref=dst, send_sem=sent, recv_sem=recv, device_id=peers[0], device_id_type=MESH).wait_recv()
+
+    def left(src, gone):
         pltpu.make_async_remote_copy(
-            src_ref=src, dst_ref=src, send_sem=sent, recv_sem=t_recv, device_id=peers[0], device_id_type=MESH).wait_send()
-
-    cd_copy.wait()
+            src_ref=src, dst_ref=src, send_sem=gone, recv_sem=t_recv, device_id=peers[0], device_id_type=MESH).wait_send()
+
+    pltpu.make_async_copy(tables.at[pl.ds(0, 2)], tables.at[pl.ds(0, 2)], local_sem.at[0]).wait()
     for column in around:
-        send(cd_smem.at[t], cd_smem.at[t], t_send, t_recv, (column, g))
-    pltpu.make_async_copy(zbuf.at[g], zbuf.at[g], local_sem.at[3]).wait()
+        send(tables.at[t], tables.at[t], t_send, t_recv, (column, g))
+    pltpu.make_async_copy(zbuf.at[g], zbuf.at[g], local_sem.at[2]).wait()
     for h in range(batch):
         for z in order[::-1]:
-            send(zbuf.at[g, h], zbuf.at[g, h], z_send, z_recv.at[g, h], (t, z))
-    send(zbuf.at[g], pbuf.at[t], p_send, p_recv.at[0], (partner, g))
+            send(zbuf.at[g, h], zbuf.at[g, h], sent, z_recv.at[without(g, z), h], (t, z))
+    send(zbuf.at[g], pbuf.at[t], sent, p_recv.at[0], (partner, g))
     for column in around:
-        send(zbuf.at[g], pbuf.at[t], p_send, p_recv.at[1], (column, g))
-    ab_copy.wait()
+        send(zbuf.at[g], pbuf.at[t], sent, p_recv.at[1], (column, g))
     int_copy.wait()
 
     def load(*at):
@@ -94,7 +88,7 @@
         return [buf[(*at, c)] for c in range(tiles_dev)]
 
     def choose(tiles, column, j):
-        cd = cd_smem[column, 0, g * groups + j]
+        cd = tables[column, 0, g * groups + j]
         chosen = tiles[0]
         for c in range(1, tiles_dev):
             chosen = jnp.where(cd == c, tiles[c], chosen)
@@ -103,7 +97,7 @@
     def term(parts, j):
         operand = jnp.concatenate(parts, axis=0)
         product = jnp.dot(operand, tile_buf[0, j], preferred_element_type=jnp.float32)
-        ab = ab_smem[0, g * groups + j]
+        ab = tables[near, 0, g * groups + j]
         return [product * (ab == a).astype(jnp.float32) for a in range(NT_DEV)]
 
     def add(left, right):
@@ -116,22 +110,22 @@
 
         @pl.when(where != g)
         def _():
-            send(rs_buf.at[h, where], sums_buf.at[h, g], rs_send, rs_recv.at[h], (t, where))
+            send(rs_buf.at[h, where], sums_buf.at[h, g], sent, rs_recv.at[h], (t, where))
 
     halves = range(batch)
     arrived(pbuf.at[partner], p_recv.at[0])
     own = [part for h in halves for part in (choose(load(zbuf, g, h), t, g), choose(load(pbuf, partner, h), t, g))]
     own = term(own, g)
-    arrived(cd_smem.at[pl.ds(0, len(around))], t_recv)
+    arrived(tables.at[pl.ds(0, len(around))], t_recv)
     for h in halves:
         for k, j in enumerate(nearest):
-            arrived(zbuf.at[j, h], z_recv.at[j, h])
-            send(zbuf.at[j, h], xbuf.at[k, h], x_send, x_recv, (partner, g))
+            arrived(zbuf.at[j, h], z_recv.at[without(j, g), h])
+            send(zbuf.at[j, h], xbuf.at[k, h], sent, x_recv, (partner, g))
             tiles = load(zbuf, j, h)
             for e, column in enumerate(around):
                 sbuf[h, k, e] = choose(tiles, column, j)
             for e, column in enumerate(around):
-                send(sbuf.at[h, k, e], abuf.at[h, k, t], a_send, a_recv.at[h, place], (column, g))
+                send(sbuf.at[h, k, e], abuf.at[h, k, t], sent, a_recv.at[h, without(place, rest[e // CORES])], (column, g))
     arrived(xbuf, x_recv)
     for k, j in enumerate(nearest):
         parts = [part for h in halves for part in (choose(load(zbuf, j, h), t, j), choose(load(xbuf, k, h), t, j))]
@@ -142,14 +136,25 @@
     arrived(pbuf.at[pl.ds(0, len(around))], p_recv.at[1])
     parts = [choose(load(pbuf, column, h), t, g) for h in halves for pair in columns for column in pair]
     base = term(parts, g)
-    for h, at in ((h, at) for h in halves for at in range(places - 1)):
-        where, pair = rising[at], columns[at]
-        start = (h * len(rising) + at) * piece
-        sums = [x[start:start + piece] for x in base]
-        arrived(abuf.at[h, :, pl.ds(0, CORES)], a_recv.at[h, where])
+    def turn(h, low, high):
+        start = (h * len(rising) + low) * piece
+        sums = [x[start:start + (high - low) * piece] for x in base]
+        for where in rising[low:high]:
+            arrived(abuf.at[h, :, pl.ds(0, CORES)], a_recv.at[h, without(where, place)])
         for k, j in enumerate(nearest):
-            sums = add(sums, term([abuf[h, k, column] for column in pair], j))
-        finish(h, where, sums)
+            sums = add(sums, term([abuf[h, k, column] for pair in columns[low:high] for column in pair], j))
+        for at in range(low, high):
+            finish(h, rising[at], [x[(at - low) * piece:(at - low + 1) * piece] for x in sums])
+
+    @pl.when(2 * g < groups)
+    def _():
+        for what in ((0, 0, 2), (0, 2, 3), (1, 0, 2), (1, 2, 3)):
+            turn(*what)
+
+    @pl.when(2 * g >= groups)
+    def _():
+        for what in ((0, 0, 1), (1, 0, 1), (0, 1, 2), (0, 2, 3), (1, 1, 2), (1, 2, 3)):
+            turn(*what)
 
     first = core == 0
     for h in halves:
@@ -161,12 +166,8 @@
         same, other = total[:pairs_dev], total[pairs_dev:]
         out_ref[h, :pairs_dev, :] = jnp.where(first, same, other)
         out_ref[h, pairs_dev:, :] = jnp.where(first, other, same)
-    left(cd_smem.at[pl.ds(0, len(around))], t_send)
-    left(zbuf.at[pl.ds(0, groups - 1)], z_send)
-    left(pbuf.at[pl.ds(0, len(around) + 1)], p_send)
-    left(xbuf, x_send)
-    left(sbuf, a_send)
-    left(rs_buf.at[:, pl.ds(0, groups - 1)], rs_send)
+    left(tables.at[pl.ds(0, len(around))], t_send)
+    left(all_sent, sent)
 
 
 def fused(groups, tiles, amplitudes, integrals, slot_cd, slot_ab):
@@ -181,6 +182,7 @@
     piece = CORES * pairs_dev
     others, around = groups - 1, CORES * (places - 1)
     dma = pltpu.SemaphoreType.DMA
+    all_sent = batch * ((2 * others + tiles - 1) * tiles_dev + others * around + others * CORES * NT_DEV)
     return pl.pallas_call(
         functools.partial(kernel, groups, places),
         out_shape=jax.ShapeDtypeStruct((batch, rows, result), jnp.bfloat16),
@@ -196,20 +198,16 @@
             pltpu.VMEM((batch, places, piece, result), jnp.float32),
             pltpu.VMEM((batch, places, piece, result), jnp.bfloat16),
             pltpu.VMEM((batch, groups, piece, result), jnp.bfloat16),
-            pltpu.SMEM((tiles, *slot_cd.shape), jnp.int32),
-            pltpu.SMEM(slot_ab.shape, jnp.int32),
-            dma((4,)),
-            dma,
-            dma((groups, batch)),
-            dma,
+            pltpu.VMEM((all_sent, pairs_dev, widths), jnp.bfloat16),
+            pltpu.SMEM((tiles + 1, *slot_cd.shape), jnp.int32),
+            dma((3,)),
+            dma,
+            dma((others, batch)),
             dma,
             dma,
             dma((2,)),
             dma,
-            dma,
-            dma,
-            dma((batch, places)),
-            dma,
+            dma((batch, places - 1)),
             dma((batch,)),
         ],
         compiler_params=pltpu.CompilerParams(collective_id=0, has_side_effects=True, vmem_limit_bytes=8 * 2**20),

time: 16.3 us -> 16.2 us (level)
  no operation moved by 1% of the time
where the time goes in v5:
time: 16.2 us; the launch traced here: 16.1 us
  Pallas kernels  15.4 us (95%)
  local copies, waits for them, and re-layouts  0.62 us (4%)
    pallas_call x1, Pallas kernels, fused(): pl.pallas_call(functools.partial(kernel, groups, places), out_shape=jax.S...  15.4 us
    unnamed x1, local copies, waits for them, and re-layouts  0.62 us

profile of v5, /device:TPU:0, one launch (start us, length us, event | category | flops | bytes accessed | tf_op | source)
XLA Modules:
  0.0 16.1 jit_solution(6571570722272731121)
XLA Ops:
  0.0 15.4 %shard_map.46 = bf16[2,16,512]{2,1,0:T(8,128)(2,1)S(1)} custom-call(bf16[2,8,1024]{2,1,0:T(8,128)(2,1)} %amp_ref.1, bf16[1,4,256,256]{3,2,1,0:T(8,128)(2,1)} %int_ref.1, s32[1,16]{1,0:T(1,128)} %cd_ref.1, s32[1,16]{1,0:T(1,128)} %ab_ref.1), custom_call_target="tpu_custom_call" | custom-call | tf_op jit(solution)/shard_map/pallas_call | solution.py:186
  15.4 0.6 %copy.6 = bf16[2,16,512]{2,1,0:T(8,128)(2,1)} copy(bf16[2,16,512]{2,1,0:T(8,128)(2,1)S(1)} %shard_map.46) | data formatting | bytes 65536

commit v6 on v5

--- a/solution.py
+++ b/solution.py
@@ -42,6 +42,8 @@
     columns = [[where * CORES + (1 - core if r else core) for r in range(CORES)] for where in rising]
     order = farthest_first(g, groups)
     nearest = order[::-1]
+    top = (g == groups - 1).astype(jnp.int32)
+    routed = [top * nearest[i] + (1 - top) * z for i, z in zip((0,2,1), nearest)]
 
     barrier = pltpu.get_barrier_semaphore()
     peers = [(t, z) for z in order] + [(column, g) for column in (partner, *around)]
@@ -51,11 +53,11 @@
     cd_copy = pltpu.make_async_copy(cd_ref, tables.at[t], local_sem.at[0])
     ab_copy = pltpu.make_async_copy(ab_ref, tables.at[near], local_sem.at[0])
     int_copy = pltpu.make_async_copy(int_ref, tile_buf, local_sem.at[1])
-    cd_copy.start()
-    ab_copy.start()
     for h in range(batch):
         for c in range(tiles_dev):
             pltpu.make_async_copy(amp_ref.at[h, :, pl.ds(c * widths, widths)], zbuf.at[g, h, c], local_sem.at[2]).start()
+    cd_copy.start()
+    ab_copy.start()
     int_copy.start()
     pl.semaphore_wait(barrier, len(peers))
 
@@ -71,13 +73,13 @@
         pltpu.make_async_remote_copy(
             src_ref=src, dst_ref=src, send_sem=gone, recv_sem=t_recv, device_id=peers[0], device_id_type=MESH).wait_send()
 
+    pltpu.make_async_copy(zbuf.at[g], zbuf.at[g], local_sem.at[2]).wait()
+    for h in range(batch):
+        for z in routed:
+            send(zbuf.at[g, h], zbuf.at[g, h], sent, z_recv.at[without(g, z), h], (t, z))
     pltpu.make_async_copy(tables.at[pl.ds(0, 2)], tables.at[pl.ds(0, 2)], local_sem.at[0]).wait()
     for column in around:
         send(tables.at[t], tables.at[t], t_send, t_recv, (column, g))
-    pltpu.make_async_copy(zbuf.at[g], zbuf.at[g], local_sem.at[2]).wait()
-    for h in range(batch):
-        for z in order[::-1]:
-            send(zbuf.at[g, h], zbuf.at[g, h], sent, z_recv.at[without(g, z), h], (t, z))
     send(zbuf.at[g], pbuf.at[t], sent, p_recv.at[0], (partner, g))
     for column in around:
         send(zbuf.at[g], pbuf.at[t], sent, p_recv.at[1], (column, g))

time: 16.2 us -> 16.1 us (level)
  no operation moved by 1% of the time
where the time goes in v6:
time: 16.1 us; the launch traced here: 16 us
  Pallas kernels  15.3 us (95%)
  local copies, waits for them, and re-layouts  0.62 us (4%)
    pallas_call x1, Pallas kernels, fused(): pl.pallas_call(functools.partial(kernel, groups, places), out_shape=jax.S...  15.3 us
    unnamed x1, local copies, waits for them, and re-layouts  0.62 us

profile of v6, /device:TPU:0, one launch (start us, length us, event | category | flops | bytes accessed | tf_op | source)
XLA Modules:
  0.0 16.0 jit_solution(13067597911008978351)
XLA Ops:
  0.0 15.3 %shard_map.46 = bf16[2,16,512]{2,1,0:T(8,128)(2,1)S(1)} custom-call(bf16[2,8,1024]{2,1,0:T(8,128)(2,1)} %amp_ref.1, bf16[1,4,256,256]{3,2,1,0:T(8,128)(2,1)} %int_ref.1, s32[1,16]{1,0:T(1,128)} %cd_ref.1, s32[1,16]{1,0:T(1,128)} %ab_ref.1), custom_call_target="tpu_custom_call" | custom-call | tf_op jit(solution)/shard_map/pallas_call | solution.py:188
  15.3 0.6 %copy.6 = bf16[2,16,512]{2,1,0:T(8,128)(2,1)} copy(bf16[2,16,512]{2,1,0:T(8,128)(2,1)S(1)} %shard_map.46) | data formatting | bytes 65536

commit v7 on v6

--- a/solution.py
+++ b/solution.py
@@ -129,11 +129,11 @@
             for e, column in enumerate(around):
                 send(sbuf.at[h, k, e], abuf.at[h, k, t], sent, a_recv.at[h, without(place, rest[e // CORES])], (column, g))
     arrived(xbuf, x_recv)
-    for k, j in enumerate(nearest):
-        parts = [part for h in halves for part in (choose(load(zbuf, j, h), t, j), choose(load(xbuf, k, h), t, j))]
-        own = add(own, term(parts, j))
     for h in halves:
-        finish(h, place, [x[h * piece:(h + 1) * piece] for x in own])
+        mine = [x[h * piece:(h + 1) * piece] for x in own]
+        for k, j in enumerate(nearest):
+            mine = add(mine, term([choose(load(zbuf, j, h), t, j), choose(load(xbuf, k, h), t, j)], j))
+        finish(h, place, mine)
 
     arrived(pbuf.at[pl.ds(0, len(around))], p_recv.at[1])
     parts = [choose(load(pbuf, column, h), t, g) for h in halves for pair in columns for column in pair]

time: 16.1 us -> 16.1 us (level)
  no operation moved by 1% of the time
where the time goes in v7:
time: 16.1 us; the launch traced here: 16 us
  Pallas kernels  15.3 us (95%)
  local copies, waits for them, and re-layouts  0.62 us (4%)
    pallas_call x1, Pallas kernels, fused(): pl.pallas_call(functools.partial(kernel, groups, places), out_shape=jax.S...  15.3 us
    unnamed x1, local copies, waits for them, and re-layouts  0.62 us

profile of v7, /device:TPU:0, one launch (start us, length us, event | category | flops | bytes accessed | tf_op | source)
XLA Modules:
  0.0 16.0 jit_solution(18141234433327498795)
XLA Ops:
  0.0 15.3 %shard_map.46 = bf16[2,16,512]{2,1,0:T(8,128)(2,1)S(1)} custom-call(bf16[2,8,1024]{2,1,0:T(8,128)(2,1)} %amp_ref.1, bf16[1,4,256,256]{3,2,1,0:T(8,128)(2,1)} %int_ref.1, s32[1,16]{1,0:T(1,128)} %cd_ref.1, s32[1,16]{1,0:T(1,128)} %ab_ref.1), custom_call_target="tpu_custom_call" | custom-call | tf_op jit(solution)/shard_map/pallas_call | solution.py:188
  15.3 0.6 %copy.6 = bf16[2,16,512]{2,1,0:T(8,128)(2,1)} copy(bf16[2,16,512]{2,1,0:T(8,128)(2,1)S(1)} %shard_map.46) | data formatting | bytes 65536
